TPU v7x, 32 devices: a whole 2x2x4 slice. The times are simulated.
32 devices in a mesh: dp: 4 (over x, core), tensor: 8 (over z, y).
Axes of the slice: x: 2, y: 2, z: 4, core: 2. Of those that a mesh axis runs over, the one named last changes fastest.
Arguments:
- tokens: bfloat16 [8192, 2048], P(('dp', 'tensor')), may hold values from -6 to 6
- attn_gain: bfloat16 [2048], replicated, may hold values from 0.099609375 to 1.8984375
- w_query: bfloat16 [2048, 2048], P(None, 'tensor'), may hold values from -0.125 to 0.125
- w_key: bfloat16 [2048, 2048], P(None, 'tensor'), may hold values from -0.125 to 0.125
- w_value: bfloat16 [2048, 2048], P(None, 'tensor'), may hold values from -0.125 to 0.125
- conv_query: bfloat16 [4, 2048], P(None, 'tensor'), may hold values from -3 to 3
- conv_key: bfloat16 [4, 2048], P(None, 'tensor'), may hold values from -3 to 3
- conv_value: bfloat16 [4, 2048], P(None, 'tensor'), may hold values from -3 to 3
- w_beta: bfloat16 [2048, 16], P(None, 'tensor'), may hold values from -0.125 to 0.125
- w_gate_out: bfloat16 [2048, 2048], P(None, 'tensor'), may hold values from -0.125 to 0.125
- head_gain: bfloat16 [128], replicated, may hold values from 0.099609375 to 1.8984375
- w_out: bfloat16 [2048, 2048], P('tensor'), may hold values from -0.25 to 0.25
- ffn_gain: bfloat16 [2048], replicated, may hold values from 0.099609375 to 1.8984375
- w_gate: bfloat16 [2048, 5632], P(None, 'tensor'), may hold values from -0.125 to 0.125
- w_up: bfloat16 [2048, 5632], P(None, 'tensor'), may hold values from -0.125 to 0.125
- w_down: bfloat16 [5632, 2048], P('tensor'), may hold values from -0.15625 to 0.15625
- seq_starts: int32 [4, 2], P('dp'), may hold values from 0 to 1536, as said below
- seq_lengths: int32 [4, 2], P('dp'), may hold values from 512 to 1024, as said below
- cotangent: bfloat16 [8192, 2048], P(('dp', 'tensor')), may hold values from -6 to 6
Outputs:
- output: bfloat16 [8192, 2048], P(('dp', 'tensor'))
- grad_tokens: float32 [8192, 2048], P(('dp', 'tensor'))
- grad_attn_gain: float32 [2048], replicated
- grad_w_query: float32 [2048, 2048], P(None, 'tensor')
- grad_w_key: float32 [2048, 2048], P(None, 'tensor')
- grad_w_value: float32 [2048, 2048], P(None, 'tensor')
- grad_conv_query: float32 [4, 2048], P(None, 'tensor')
- grad_conv_key: float32 [4, 2048], P(None, 'tensor')
- grad_conv_value: float32 [4, 2048], P(None, 'tensor')
- grad_w_beta: float32 [2048, 16], P(None, 'tensor')
- grad_w_gate_out: float32 [2048, 2048], P(None, 'tensor')
- grad_head_gain: float32 [128], replicated
- grad_w_out: float32 [2048, 2048], P('tensor')
- grad_ffn_gain: float32 [2048], replicated
- grad_w_gate: float32 [2048, 5632], P(None, 'tensor')
- grad_w_up: float32 [2048, 5632], P(None, 'tensor')
- grad_w_down: float32 [5632, 2048], P('tensor')
Inputs may be any that keep to these rules, and one draw needn't show every extreme that they name: `seq_lengths`: each shard holds 2 sequences; the first shard's first sequence has 1024 tokens and its last one 2048 // 4. `seq_starts`: the sequences of a shard lie in order within its 2048 slots and do not intersect, the first starting at slot 0; the other slots are padding. The first shard's last sequence ends at its last slot.
All inputs are finite; a program needn't handle non-finite values.
Results may differ from a plain program's by a relative error of at most 0.02.
Values may be sent and summed in bfloat16 or wider, within the bound.
A program may use at most 320 MiB of HBM per device.

v0:
```python
import jax
import jax.numpy as jnp
from jax import lax
from jax.sharding import PartitionSpec as P

STRETCH = 64
highest = lax.Precision.HIGHEST


def round_pass(value):
    return lax.optimization_barrier(value.astype(jnp.bfloat16)).astype(jnp.float32)


def round_keep(value):
    return (round_pass(value), None)


def round_grad(kept, grad):
    return (grad,)


def make_rounding():
    rounder = jax.custom_vjp(round_pass)
    rounder.defvjp(round_keep, round_grad)
    return rounder


def positions(starts, lengths, slot_count):
    places = jnp.arange(slot_count, dtype=jnp.int32)
    begun = (places[:, None] >= starts[None, :]).astype(jnp.int32)
    ended = (places[:, None] >= (starts + lengths)[None, :]).astype(jnp.int32)
    segment = jnp.sum(begun + ended, axis=1)
    live = (segment % 2).astype(jnp.float32)
    return (segment, live)


def short_conv(inputs, taps, segment):
    result = inputs * taps[0]
    for offset in range(1, taps.shape[0]):
        moved = jnp.concatenate(
            [jnp.zeros((offset, inputs.shape[1]), jnp.float32), inputs[:-offset]], 0
        )
        earlier = jnp.concatenate([jnp.full((offset,), -1, jnp.int32), segment[:-offset]], 0)
        result = result + moved * taps[offset] * (earlier == segment).astype(jnp.float32)[:, None]
    return result


def unit_rows(inputs):
    return inputs * lax.rsqrt(jnp.sum(inputs * inputs, axis=-1, keepdims=True) + 1e-06)


def delta_rule(queries, key_rows, values, strength, segment):
    slot_count, head_width = queries.shape
    blocks = slot_count // STRETCH
    query_blocks = (queries * head_width ** (-0.5)).reshape(blocks, STRETCH, head_width)
    key_blocks = key_rows.reshape(blocks, STRETCH, head_width)
    value_blocks = values.reshape(blocks, STRETCH, head_width)
    beta_blocks = strength.reshape(blocks, STRETCH)
    seg_blocks = segment.reshape(blocks, STRETCH)
    same_seg = (seg_blocks[:, :, None] == seg_blocks[:, None, :]).astype(jnp.float32)
    places = jnp.arange(STRETCH)
    strict = (places[:, None] > places[None, :]).astype(jnp.float32)
    inclusive = (places[:, None] >= places[None, :]).astype(jnp.float32)
    key_inner = jnp.einsum("nik,njk->nij", key_blocks, key_blocks, precision=highest)
    system = (
        jnp.eye(STRETCH, dtype=jnp.float32)[None]
        + beta_blocks[:, :, None] * key_inner * same_seg * strict
    )
    weighted = lax.linalg.triangular_solve(
        system, beta_blocks[:, :, None] * key_blocks, left_side=True, lower=True, unit_diagonal=True
    )
    updates = lax.linalg.triangular_solve(
        system,
        beta_blocks[:, :, None] * value_blocks,
        left_side=True,
        lower=True,
        unit_diagonal=True,
    )
    within = (
        jnp.einsum("nik,njk->nij", query_blocks, key_blocks, precision=highest)
        * same_seg
        * inclusive
    )
    earlier_last = jnp.concatenate([jnp.full((1,), -1, jnp.int32), seg_blocks[:-1, STRETCH - 1]], 0)
    continued = (seg_blocks[:, 0] == earlier_last).astype(jnp.float32)
    carried = same_seg[:, :, 0] * continued[:, None]
    ending = same_seg[:, :, STRETCH - 1]
    kept_state = continued * same_seg[:, 0, STRETCH - 1]

    def advance(memory, pieces):
        query_part, key_part, weight_part, update_part, mixing, carry_part, end_part, keep_part = (
            pieces
        )
        change = update_part - carry_part[:, None] * jnp.dot(
            weight_part, memory.T, precision=highest
        )
        result = carry_part[:, None] * jnp.dot(query_part, memory.T, precision=highest) + jnp.dot(
            mixing, change, precision=highest
        )
        memory = keep_part * memory + jnp.dot(
            (end_part[:, None] * change).T, key_part, precision=highest
        )
        return (memory, result)

    start_memory = jnp.zeros((head_width, head_width), jnp.float32)
    last_memory, outputs = lax.scan(
        jax.checkpoint(advance),
        start_memory,
        (query_blocks, key_blocks, weighted, updates, within, carried, ending, kept_state),
    )
    return outputs.reshape(slot_count, head_width)


def mixer_local(
    proj_query,
    proj_key,
    proj_value,
    proj_beta,
    proj_gate,
    taps_query,
    taps_key,
    taps_value,
    gain_head,
    segment,
    live,
    rounder,
):
    slot_count = proj_query.shape[0]
    head_count = proj_beta.shape[1]
    head_width = proj_query.shape[1] // head_count

    def feature(projected, taps):
        return jax.nn.silu(short_conv(projected, taps, segment)).reshape(
            slot_count, head_count, head_width
        )

    queries = rounder(unit_rows(feature(proj_query, taps_query)))
    key_rows = rounder(unit_rows(feature(proj_key, taps_key)))
    values = rounder(feature(proj_value, taps_value))
    strength = jax.nn.sigmoid(proj_beta)
    delta_out = jax.vmap(delta_rule, in_axes=(1, 1, 1, 1, None), out_axes=1)(
        queries, key_rows, values, strength, segment
    )
    head_normed = (
        delta_out
        * lax.rsqrt(jnp.mean(delta_out * delta_out, axis=-1, keepdims=True) + 1e-05)
        * gain_head
    )
    gated = (
        head_normed
        * jax.nn.silu(proj_gate.reshape(slot_count, head_count, head_width))
        * live[:, None, None]
    )
    return gated.reshape(slot_count, head_count * head_width)


def norm_back(inputs, scale, gain, grad_normed):
    weighted_grad = gain * grad_normed
    inner = jnp.mean(weighted_grad * inputs, axis=1, keepdims=True)
    grad_inputs = scale * weighted_grad - inputs * scale * scale * scale * inner
    grad_gain = jnp.sum(grad_normed * inputs * scale, axis=0)
    return (grad_inputs, grad_gain)


def shards(
    tokens,
    attn_gain,
    w_query,
    w_key,
    w_value,
    conv_query,
    conv_key,
    conv_value,
    w_beta,
    w_gate_out,
    head_gain,
    w_out,
    ffn_gain,
    w_gate,
    w_up,
    w_down,
    seq_starts,
    seq_lengths,
    cotangent,
):
    row_count = tokens.shape[0]
    slot_count = row_count * lax.axis_size("tensor")
    segment, live = positions(seq_starts[0], seq_lengths[0], slot_count)
    rounder = make_rounding()
    inputs = tokens.astype(jnp.float32)
    gain_first = attn_gain.astype(jnp.float32)
    scale_first = lax.rsqrt(jnp.mean(inputs * inputs, axis=1, keepdims=True) + 1e-06)
    normed = (inputs * scale_first * gain_first).astype(jnp.bfloat16)
    normed_full = lax.all_gather(normed, "tensor", axis=0, tiled=True)
    mixer_weights = (w_query, w_key, w_value, w_beta, w_gate_out)
    projected = [
        jnp.dot(normed_full, weight, preferred_element_type=jnp.float32) for weight in mixer_weights
    ]

    def mixer_piece(
        proj_query,
        proj_key,
        proj_value,
        proj_beta,
        proj_gate,
        taps_query,
        taps_key,
        taps_value,
        gain_head,
    ):
        return mixer_local(
            proj_query,
            proj_key,
            proj_value,
            proj_beta,
            proj_gate,
            taps_query,
            taps_key,
            taps_value,
            gain_head,
            segment,
            live,
            rounder,
        )

    mixed, mixer_pullback = jax.vjp(
        mixer_piece,
        projected[0],
        projected[1],
        projected[2],
        projected[3],
        projected[4],
        conv_query.astype(jnp.float32),
        conv_key.astype(jnp.float32),
        conv_value.astype(jnp.float32),
        head_gain.astype(jnp.float32),
    )
    mixed_low = mixed.astype(jnp.bfloat16)
    attended = lax.psum_scatter(
        jnp.dot(mixed_low, w_out, preferred_element_type=jnp.float32).astype(jnp.bfloat16),
        "tensor",
        scatter_dimension=0,
        tiled=True,
    ).astype(jnp.float32)
    resid = inputs + attended
    gain_second = ffn_gain.astype(jnp.float32)
    scale_second = lax.rsqrt(jnp.mean(resid * resid, axis=1, keepdims=True) + 1e-06)
    ffn_in = (resid * scale_second * gain_second).astype(jnp.bfloat16)
    ffn_full = lax.all_gather(ffn_in, "tensor", axis=0, tiled=True)
    gate_pre = jnp.dot(ffn_full, w_gate, preferred_element_type=jnp.float32)
    up_pre = jnp.dot(ffn_full, w_up, preferred_element_type=jnp.float32)
    sigmoid_gate = jax.nn.sigmoid(gate_pre)
    silu_gate = gate_pre * sigmoid_gate
    hidden = (silu_gate * up_pre).astype(jnp.bfloat16)
    output = resid + lax.psum_scatter(
        jnp.dot(hidden, w_down, preferred_element_type=jnp.float32).astype(jnp.bfloat16),
        "tensor",
        scatter_dimension=0,
        tiled=True,
    ).astype(jnp.float32)
    grad_full = lax.all_gather(cotangent, "tensor", axis=0, tiled=True)
    grad_hidden = jnp.einsum("sd,fd->sf", grad_full, w_down, preferred_element_type=jnp.float32)
    grad_w_down = jnp.einsum("sf,sd->fd", hidden, grad_full, preferred_element_type=jnp.float32)
    grad_gate = (
        grad_hidden * up_pre * sigmoid_gate * (1.0 + gate_pre * (1.0 - sigmoid_gate))
    ).astype(jnp.bfloat16)
    grad_up = (grad_hidden * silu_gate).astype(jnp.bfloat16)
    grad_w_gate = jnp.einsum("sd,sf->df", ffn_full, grad_gate, preferred_element_type=jnp.float32)
    grad_w_up = jnp.einsum("sd,sf->df", ffn_full, grad_up, preferred_element_type=jnp.float32)
    grad_ffn_in = lax.psum_scatter(
        (
            jnp.einsum("sf,df->sd", grad_gate, w_gate, preferred_element_type=jnp.float32)
            + jnp.einsum("sf,df->sd", grad_up, w_up, preferred_element_type=jnp.float32)
        ).astype(jnp.bfloat16),
        "tensor",
        scatter_dimension=0,
        tiled=True,
    ).astype(jnp.float32)
    grad_through, grad_ffn_gain = norm_back(resid, scale_second, gain_second, grad_ffn_in)
    grad_resid = cotangent.astype(jnp.float32) + grad_through
    grad_attended = lax.all_gather(grad_resid.astype(jnp.bfloat16), "tensor", axis=0, tiled=True)
    grad_mixed = jnp.einsum("sd,hd->sh", grad_attended, w_out, preferred_element_type=jnp.float32)
    grad_w_out = jnp.einsum(
        "sh,sd->hd", mixed_low, grad_attended, preferred_element_type=jnp.float32
    )
    pulled = mixer_pullback(grad_mixed)
    grad_projected = [pulled[index].astype(jnp.bfloat16) for index in range(5)]
    grad_mixer_weights = [
        jnp.einsum("sd,sh->dh", normed_full, grad_part, preferred_element_type=jnp.float32)
        for grad_part in grad_projected
    ]
    summed = jnp.zeros((row_count * lax.axis_size("tensor"), normed.shape[1]), jnp.float32)
    for grad_part, weight in zip(grad_projected, mixer_weights):
        summed = summed + jnp.einsum(
            "sh,dh->sd", grad_part, weight, preferred_element_type=jnp.float32
        )
    grad_normed = lax.psum_scatter(
        summed.astype(jnp.bfloat16), "tensor", scatter_dimension=0, tiled=True
    ).astype(jnp.float32)
    grad_first, grad_attn_gain = norm_back(inputs, scale_first, gain_first, grad_normed)
    grad_tokens = grad_resid + grad_first
    grad_attn_gain, grad_ffn_gain, grad_head_gain = lax.psum(
        (grad_attn_gain, grad_ffn_gain, pulled[8]), ("dp", "tensor")
    )
    mixer_grads = (
        grad_mixer_weights[0],
        grad_mixer_weights[1],
        grad_mixer_weights[2],
        pulled[5],
        pulled[6],
        pulled[7],
        grad_mixer_weights[3],
        grad_mixer_weights[4],
        grad_w_out,
    )
    summed_all = (
        lax.psum(mixer_grads[0].astype(jnp.bfloat16), "dp").astype(jnp.float32),
        lax.psum(mixer_grads[1].astype(jnp.bfloat16), "dp").astype(jnp.float32),
        lax.psum(mixer_grads[2].astype(jnp.bfloat16), "dp").astype(jnp.float32),
        lax.psum(mixer_grads[3].astype(jnp.bfloat16), "dp").astype(jnp.float32),
        lax.psum(mixer_grads[4].astype(jnp.bfloat16), "dp").astype(jnp.float32),
        lax.psum(mixer_grads[5].astype(jnp.bfloat16), "dp").astype(jnp.float32),
        lax.psum(mixer_grads[6].astype(jnp.bfloat16), "dp").astype(jnp.float32),
        lax.psum(mixer_grads[7].astype(jnp.bfloat16), "dp").astype(jnp.float32),
        lax.psum(mixer_grads[8].astype(jnp.bfloat16), "dp").astype(jnp.float32),
        lax.psum(grad_w_gate.astype(jnp.bfloat16), "dp").astype(jnp.float32),
        lax.psum(grad_w_up.astype(jnp.bfloat16), "dp").astype(jnp.float32),
        lax.psum(grad_w_down.astype(jnp.bfloat16), "dp").astype(jnp.float32),
    )
    mixer_grads = summed_all[:9]
    grad_w_gate, grad_w_up, grad_w_down = (summed_all[9], summed_all[10], summed_all[11])
    return (
        output.astype(jnp.bfloat16),
        grad_tokens,
        grad_attn_gain,
        mixer_grads[0],
        mixer_grads[1],
        mixer_grads[2],
        mixer_grads[3],
        mixer_grads[4],
        mixer_grads[5],
        mixer_grads[6],
        mixer_grads[7],
        grad_head_gain,
        mixer_grads[8],
        grad_ffn_gain,
        grad_w_gate,
        grad_w_up,
        grad_w_down,
    )


def solution(mesh):
    placed = (
        P(("dp", "tensor"), None),
        P(),
        P(None, "tensor"),
        P(None, "tensor"),
        P(None, "tensor"),
        P(None, "tensor"),
        P(None, "tensor"),
        P(None, "tensor"),
        P(None, "tensor"),
        P(None, "tensor"),
        P(),
        P("tensor", None),
        P(),
        P(None, "tensor"),
        P(None, "tensor"),
        P("tensor", None),
        P("dp", None),
        P("dp", None),
        P(("dp", "tensor"), None),
    )
    return jax.shard_map(
        shards,
        mesh=mesh,
        in_specs=placed,
        out_specs=(
            P(("dp", "tensor"), None),
            P(("dp", "tensor"), None),
            P(),
            P(None, "tensor"),
            P(None, "tensor"),
            P(None, "tensor"),
            P(None, "tensor"),
            P(None, "tensor"),
            P(None, "tensor"),
            P(None, "tensor"),
            P(None, "tensor"),
            P(),
            P("tensor", None),
            P(),
            P(None, "tensor"),
            P(None, "tensor"),
            P("tensor", None),
        ),
        check_vma=False,
    )
```

profile of v0, /device:TPU:0, one launch (start us, length us, event | category | flops | bytes accessed | tf_op | source)
XLA Modules:
  0.0 2470.4 jit_solution(2814759676212930123)
XLA Ops:
  14.5 4.0 copy.315
  21.9 118.7 %all-gather.5.cloned.1.call-done = bf16[2048,2048]{1,0:T(8,128)(2,1)} async-done(((bf16[256,2048]{1,0:T(8,128)(2,1)}), bf16[2048,2048]{1,0:T(8,128)(2,1)}) %all-gather.5.cloned.1.call-update) | async-done | bytes 8388624 | tf_op jit(solution)/shard_map/all_gather | solution.py:194
  140.6 5.7 fusion.50
  147.0 7.3 fusion.140
  157.4 6.0 fusion.137
  171.2 6.1 fusion.138
  177.3 6.5 fusion.135
  184.0 6.3 multiply_reduce_fusion.16
  211.6 3.9 copy.322
  215.5 5.6 copy.314
  224.4 9.4 multiply_bitcast_fusion
  233.7 134.0 %custom-call.14 = f32[2,32,1,64,64]{1,3,4,2,0:T(8,128)} custom-call(f32[2,32,1,64,64]{1,4,3,2,0:T(8,128)} %get-tuple-element.855), custom_call_target="InvertDiagBlocksLowerTriangular" | custom-call | tf_op jit(solution)/shard_map/jvp(vmap())/triangular_solve/custom-call.1 | solution.py:72
  367.7 5.6 copy.318
  373.4 4.3 fusion.61
  383.7 4.1 copy.327
  389.4 235.3 %while.40 = (s32[]{:T(128)}, f32[2,128,128]{2,1,0:T(8,128)S(1)}, f32[32,2,64,128]{3,2,0,1:T(8,128)}, f32[32,2,128,128]{3,2,1,0:T(8,128)}, f32[32]{0:T(128)S(1)},...) while((s32[]{:T(128)}, f32[2,128,128]{2,1,0:T(8,128)S(1)}, ...), condition=%wide.region_5.7_spmd.clone, body=%wide.region_4.6_spmd.clone.sunk | while | flops 88358912 | bytes 1512373 | solution.py:106
  632.4 7.3 convolution_convert_fusion.1
  640.4 146.7 %reduce-scatter.5.cloned.1.call-done = bf16[256,2048]{1,0:T(8,128)(2,1)} async-done(((bf16[2048,2048]{1,0:T(8,128)(2,1)}), bf16[256,2048]{1,0:T(8,128)(2,1)}) %reduce-scatter.5.cloned.1.call-update) | async-done | bytes 1048592 | tf_op jit(solution)/shard_map/reduce_scatter | solution.py:239
  791.4 123.5 %all-gather.7.cloned.1.call-done = bf16[2048,2048]{1,0:T(8,128)(2,1)} async-done(((bf16[256,2048]{1,0:T(8,128)(2,1)}), bf16[2048,2048]{1,0:T(8,128)(2,1)}) %all-gather.7.cloned.1.call-update) | async-done | bytes 8388624 | tf_op jit(solution)/shard_map/all_gather | solution.py:249
  914.9 11.4 fusion.142
  926.2 8.0 fusion.141
  934.2 106.0 %all-gather.9.cloned.1.call-done = bf16[2048,2048]{1,0:T(8,128)(2,1)} async-done(((bf16[256,2048]{1,0:T(8,128)(2,1)}), bf16[2048,2048]{1,0:T(8,128)(2,1)}) %all-gather.9.cloned.1.call-update) | async-done | bytes 8388624 | tf_op jit(solution)/shard_map/all_gather | solution.py:261
  1040.2 14.7 multiply_convert_fusion
  1054.9 10.7 fusion.143
  1065.6 12.5 add_convert_fusion.1
  1078.2 147.3 %reduce-scatter.9.cloned.1.call-done = bf16[256,2048]{1,0:T(8,128)(2,1)} async-done(((bf16[2048,2048]{1,0:T(8,128)(2,1)}), bf16[256,2048]{1,0:T(8,128)(2,1)}) %reduce-scatter.9.cloned.1.call-update) | async-done | bytes 1048592 | tf_op jit(solution)/shard_map/reduce_scatter | solution.py:270
  1235.1 4.6 copy.348
  1239.7 5.4 copy.337
  1245.1 10.7 convolution_convert_fusion.2
  1255.9 11.0 convolution_convert_fusion.3
  1266.9 7.5 convolution_convert_fusion.4
  1274.4 82.0 %all-gather.11.cloned.1.call-done = bf16[2048,2048]{1,0:T(8,128)(2,1)} async-done(((bf16[256,2048]{1,0:T(8,128)(2,1)}), bf16[2048,2048]{1,0:T(8,128)(2,1)}) %all-gather.11.cloned.1.call-update) | async-done | bytes 8388624 | tf_op jit(solution)/shard_map/all_gather | solution.py:281
  1356.4 7.4 fusion.144
  1366.7 5.4 multiply_reduce_fusion.1
  1382.8 377.5 %while.41 = (s32[]{:T(128)}, f32[2,128,128]{2,1,0:T(8,128)S(1)}, f32[32,2,64,128]{3,2,0,1:T(8,128)}, f32[32,2,64,128]{3,2,0,1:T(8,128)}, f32[32,2,64,128]{3,2,1,...) while((s32[]{:T(128)}, f32[2,128,128]{2,1,0:T(8,128)S(1)}, ...), condition=%wide.region_14.16_spmd.clone, body=%wide.region_13.15_spmd.clone.sunk | while | flops 201637888 | bytes 3902479 | solution.py:106
  1760.4 5.8 fusion.92
  1769.8 3.7 fusion.62
  1773.5 3.8 broadcast_multiply_fusion.1
  1784.0 5.6 copy.359
  1789.6 5.6 copy.354
  1795.2 8.1 broadcast_multiply_fusion
  1803.3 4.5 copy.361
  1807.9 5.1 fusion.148
  1824.4 10.2 fusion.79
  1849.6 8.3 multiply_reduce_fusion.9
  1861.7 6.9 multiply_reduce_fusion.4
  1868.7 3.7 slice_multiply_fusion.1
  1878.9 4.1 multiply_reduce_fusion.2
  1885.6 7.4 convolution_convert_fusion.5
  1893.1 3.7 convolution_convert_fusion.6
  1896.8 4.1 convolution_convert_fusion.7
  1909.0 9.0 fusion.133
  1918.0 8.2 fusion.150
  1926.2 8.2 fusion.151
  1934.4 8.3 fusion.145
  1942.7 26.4 %add_convert_fusion = bf16[2048,2048]{1,0:T(8,128)(2,1)} fusion(f32[2048,2048]{1,0:T(8,128)} %fusion.133, f32[2048,2048]{1,0:T(8,128)} %fusion.151, f32[2048,2048]{1,0:T(8,128)} %fusion.145, f32[2048,2048]{1,0:T(8,128)} %fusion.150, bf16[2048,256]{0,1:T(8,128)(2,1)S(1)} %bitcast.470, bf16[2048,256]{1,0:T(8,128)(2,1)S(1)} %copy-done.58), kind=kOutput, calls=%fused_computation.70 | convolution fusion | flops 2168455168 | bytes 77594624 | tf_op jit(solution)/shard_map/sh,dh->sd/dot_general | solution.py:294
  1969.4 10.9 convolution_convert_fusion
  1980.3 4.7 convolution_convert_fusion.10
  1985.1 12.4 all-reduce.33
  1999.9 151.3 %all-reduce.37.cloned.1.call-done = (bf16[2048,256]{1,0:T(8,128)(2,1)}, bf16[2048,256]{1,0:T(8,128)(2,1)}, bf16[2048,256]{1,0:T(8,128)(2,1)}, bf16[2048,256]{1,0...) async-done(((bf16[2048,256]{1,0:T(8,128)(2,1)}, bf16[2048,256]{1,0:T(8,128)(2,1)}, ...) | async-done | bytes 13893648 | tf_op jit(solution)/shard_map/psum | solution.py:317
  2171.1 133.0 %reduce-scatter.11.cloned.1.call-done = bf16[256,2048]{1,0:T(8,128)(2,1)} async-done(((bf16[2048,2048]{1,0:T(8,128)(2,1)}), bf16[256,2048]{1,0:T(8,128)(2,1)}) %reduce-scatter.11.cloned.1.call-update) | async-done | bytes 1048592 | tf_op jit(solution)/shard_map/reduce_scatter | solution.py:297
  2306.3 43.1 %all-reduce.32 = (f32[2048]{0:T(1024)}, f32[128]{0:T(128)}, f32[2048]{0:T(1024)}) all-reduce(f32[2048]{0:T(1024)S(1)} %get-tuple-element.718, f32[128]{0:T(128)S(1)} %copy-done.130, f32[2048]{0:T(1024)S(1)} %copy-done.95), channel_id=1, replica_groups=mesh['dp'=4,'tensor'=8] {'dp','tensor'}, use_global_device_ids=true, to_apply=%region_23.27 | all-reduce | flops 4224 | bytes 33792 | tf_op jit(solution)/shard_map/psum | solution.py:302
  2349.5 107.7 %reduce-scatter.7.cloned.1.call-done = bf16[256,2048]{1,0:T(8,128)(2,1)} async-done(((bf16[2048,2048]{1,0:T(8,128)(2,1)}), bf16[256,2048]{1,0:T(8,128)(2,1)}) %reduce-scatter.7.cloned.1.call-update) | async-done | bytes 1048592 | tf_op jit(solution)/shard_map/reduce_scatter | solution.py:255
  2457.2 6.4 fusion.55
  (1199 shorter events, 781.9 us)
Async XLA Ops:
  7.2 1033.0 %copy-start = (bf16[704,2048]{1,0:T(8,128)(2,1)S(1)}, bf16[704,2048]{1,0:T(8,128)(2,1)}, u32[]{:S(2)}) copy-start(bf16[704,2048]{1,0:T(8,128)(2,1)} %param.44) | copy-start | bytes 8650756
  7.2 133.3 %all-gather.5.cloned.1.call-start = ((), (), s32[]{:S(2)}) async-start(), calls=%async_computation.4 | async-start | bytes 9437184 | tf_op jit(solution)/shard_map/all_gather | solution.py:194
  12.8 774.3 %reduce-scatter.5.cloned.1.call-start = ((), (), s32[]{:S(2)}) async-start(), calls=%async_computation.5 | async-start | bytes 9437184 | tf_op jit(solution)/shard_map/reduce_scatter | solution.py:239
  13.2 127.4 %copy-start.93 = (bf16[2048,2]{0,1:T(2,128)(2,1)S(1)}, bf16[2048,2]{0,1:T(2,128)(2,1)}, u32[]{:S(2)}) copy-start(bf16[2048,2]{0,1:T(2,128)(2,1)} %param.37) | copy-start | bytes 24580
  19.5 204.8 %copy-start.69 = (f32[64,64]{1,0:T(8,128)}, f32[64,64]{1,0:T(8,128)S(1)}, u32[]{:S(2)}) copy-start(f32[64,64]{1,0:T(8,128)S(1)} %fusion.110) | copy-start | bytes 49156
  19.5 204.8 %copy-start.73 = (f32[64,64]{1,0:T(8,128)}, f32[64,64]{1,0:T(8,128)S(1)}, u32[]{:S(2)}) copy-start(f32[64,64]{1,0:T(8,128)S(1)} %fusion.109) | copy-start | bytes 49156
  20.0 163.9 %copy-start.102 = (f32[1,256]{1,0:T(1,128)}, f32[1,256]{1,0:T(1,128)S(1)}, u32[]{:S(2)}) copy-start(f32[1,256]{1,0:T(1,128)S(1)} %get-tuple-element.879) | copy-start | bytes 3076
  20.0 163.9 %copy-start.106 = (f32[1,256]{1,0:T(1,128)}, f32[1,256]{1,0:T(1,128)S(1)}, u32[]{:S(2)}) copy-start(f32[1,256]{1,0:T(1,128)S(1)} %get-tuple-element.881) | copy-start | bytes 3076
  20.0 163.9 %copy-start.108 = (f32[1,256]{1,0:T(1,128)}, f32[1,256]{1,0:T(1,128)S(1)}, u32[]{:S(2)}) copy-start(f32[1,256]{1,0:T(1,128)S(1)} %get-tuple-element.880) | copy-start | bytes 3076
  20.0 163.9 %copy-start.120 = (f32[1,256]{1,0:T(1,128)}, f32[1,256]{1,0:T(1,128)S(1)}, u32[]{:S(2)}) copy-start(f32[1,256]{1,0:T(1,128)S(1)} %get-tuple-element.882) | copy-start | bytes 3076
  20.0 163.8 %copy-start.104 = (f32[1,256]{1,0:T(1,128)}, f32[1,256]{1,0:T(1,128)S(1)}, u32[]{:S(2)}) copy-start(f32[1,256]{1,0:T(1,128)S(1)} %get-tuple-element.887) | copy-start | bytes 3076
  20.1 163.8 %copy-start.112 = (f32[1,256]{1,0:T(1,128)}, f32[1,256]{1,0:T(1,128)S(1)}, u32[]{:S(2)}) copy-start(f32[1,256]{1,0:T(1,128)S(1)} %get-tuple-element.889) | copy-start | bytes 3076
  20.1 163.8 %copy-start.114 = (f32[1,256]{1,0:T(1,128)}, f32[1,256]{1,0:T(1,128)S(1)}, u32[]{:S(2)}) copy-start(f32[1,256]{1,0:T(1,128)S(1)} %get-tuple-element.888) | copy-start | bytes 3076
  20.1 163.8 %copy-start.124 = (f32[1,256]{1,0:T(1,128)}, f32[1,256]{1,0:T(1,128)S(1)}, u32[]{:S(2)}) copy-start(f32[1,256]{1,0:T(1,128)S(1)} %get-tuple-element.890) | copy-start | bytes 3076
  20.1 143.4 %copy-start.110 = (f32[1,256]{1,0:T(1,128)}, f32[1,256]{1,0:T(1,128)S(1)}, u32[]{:S(2)}) copy-start(f32[1,256]{1,0:T(1,128)S(1)} %get-tuple-element.883) | copy-start | bytes 3076
  20.1 143.4 %copy-start.116 = (f32[1,256]{1,0:T(1,128)}, f32[1,256]{1,0:T(1,128)S(1)}, u32[]{:S(2)}) copy-start(f32[1,256]{1,0:T(1,128)S(1)} %get-tuple-element.884) | copy-start | bytes 3076
  20.1 143.4 %copy-start.118 = (f32[1,256]{1,0:T(1,128)}, f32[1,256]{1,0:T(1,128)S(1)}, u32[]{:S(2)}) copy-start(f32[1,256]{1,0:T(1,128)S(1)} %get-tuple-element.885) | copy-start | bytes 3076
  20.1 143.4 %copy-start.122 = (f32[1,256]{1,0:T(1,128)}, f32[1,256]{1,0:T(1,128)S(1)}, u32[]{:S(2)}) copy-start(f32[1,256]{1,0:T(1,128)S(1)} %get-tuple-element.886) | copy-start | bytes 3076
  20.2 204.1 %copy-start.91 = (pred[64,64]{1,0:T(8,128)(4,1)}, pred[64,64]{1,0:T(8,128)(4,1)S(1)}, u32[]{:S(2)}) copy-start(pred[64,64]{1,0:T(8,128)(4,1)S(1)} %iota_compare_fusion.1) | copy-start | bytes 12292
  21.0 162.9 %copy-start.85 = (f32[2048]{0:T(1024)}, f32[2048]{0:T(1024)S(1)}, u32[]{:S(2)}) copy-start(f32[2048]{0:T(1024)S(1)} %get-tuple-element.876) | copy-start | bytes 24580
  21.0 162.9 %copy-start.87 = (f32[2048]{0:T(1024)}, f32[2048]{0:T(1024)S(1)}, u32[]{:S(2)}) copy-start(f32[2048]{0:T(1024)S(1)} %get-tuple-element.878) | copy-start | bytes 24580
  21.1 162.9 %copy-start.89 = (f32[2048]{0:T(1024)}, f32[2048]{0:T(1024)S(1)}, u32[]{:S(2)}) copy-start(f32[2048]{0:T(1024)S(1)} %get-tuple-element.877) | copy-start | bytes 24580
  146.9 230.8 %copy-start.56 = (f32[2,32,64]{2,1,0:T(8,128)}, f32[2,32,64]{2,1,0:T(8,128)S(1)}, u32[]{:S(2)}) copy-start(f32[2,32,64]{2,1,0:T(8,128)S(1)} %mul.1002) | copy-start | bytes 49156
  147.0 77.3 %copy-start.67 = (f32[2,32,64]{1,2,0:T(8,128)}, f32[2,32,64]{1,2,0:T(8,128)S(1)}, u32[]{:S(2)}) copy-start(f32[2,32,64]{1,2,0:T(8,128)S(1)} %copy.312) | copy-start | bytes 49156
  639.8 275.1 %all-gather.7.cloned.1.call-start = ((), (), s32[]{:S(2)}) async-start(), calls=%async_computation.6 | async-start | bytes 9437184 | tf_op jit(solution)/shard_map/all_gather | solution.py:249
  640.4 588.5 %copy-start.75 = (f32[2048]{0:T(1024)}, f32[2048]{0:T(1024)S(1)}, u32[]{:S(2)}) copy-start(f32[2048]{0:T(1024)S(1)} %convert_element_type.274) | copy-start | bytes 24580
  789.3 439.6 %copy-start.96 = (f32[256]{0:T(256)}, f32[256]{0:T(256)S(1)}, u32[]{:S(2)}) copy-start(f32[256]{0:T(256)S(1)} %add_rsqrt_fusion.2) | copy-start | bytes 3076
  790.8 249.4 %all-gather.9.cloned.1.call-start = ((), (), s32[]{:S(2)}) async-start(), calls=%async_computation.8 | async-start | bytes 9437184 | tf_op jit(solution)/shard_map/all_gather | solution.py:261
  791.4 434.2 %reduce-scatter.9.cloned.1.call-start = ((), (), s32[]{:S(2)}) async-start(), calls=%async_computation.9 | async-start | bytes 9437184 | tf_op jit(solution)/shard_map/reduce_scatter | solution.py:270
  914.9 11.4 copy-start.132
  914.9 11.4 copy-start.133
  1040.2 14.7 copy-start.134
  1054.9 10.7 copy-start.138
  1054.9 10.7 copy-start.140
  1054.9 10.7 copy-start.135
  1078.2 278.2 %all-gather.11.cloned.1.call-start = ((), (), s32[]{:S(2)}) async-start(), calls=%async_computation.10 | async-start | bytes 9437184 | tf_op jit(solution)/shard_map/all_gather | solution.py:281
  1232.3 918.9 %all-reduce.37.cloned.1.call-start = ((), (), s32[]{:S(2)}) async-start(), calls=%async_computation.12 | async-start | bytes 27787264 | tf_op jit(solution)/shard_map/psum | solution.py:317
  1245.1 10.7 copy-start.139
  1245.1 21.7 slice-start.2
  1255.9 11.0 slice-start.3
  1255.9 11.0 copy-start.141
  1824.3 16.1 copy-start.80
  1824.4 16.1 copy-start.82
  1849.6 8.3 copy-start.125
  1884.0 16.9 copy-start.49
  1884.0 9.0 slice-start
  1885.6 19.0 copy-start.51
  1908.3 395.8 %reduce-scatter.11.cloned.1.call-start = ((), (), s32[]{:S(2)}) async-start(), calls=%async_computation.11 | async-start | bytes 9437184 | tf_op jit(solution)/shard_map/reduce_scatter | solution.py:297
  1909.0 9.0 copy-start.50
  1909.0 9.0 copy-start.60
  1918.0 8.2 copy-start.48
  1918.0 8.2 copy-start.61
  1926.2 8.2 copy-start.52
  1926.2 8.2 copy-start.62
  1934.4 8.3 copy-start.46
  1934.4 8.3 copy-start.58
  1969.1 488.0 %reduce-scatter.7.cloned.1.call-start = ((), (), s32[]{:S(2)}) async-start(), calls=%async_computation.7 | async-start | bytes 9437184 | tf_op jit(solution)/shard_map/reduce_scatter | solution.py:255
  2167.8 136.3 %copy-start.84 = (f32[2048]{0:T(1024)S(1)}, f32[2048]{0:T(1024)}, u32[]{:S(2)}) copy-start(f32[2048]{0:T(1024)} %copy-done.83) | copy-start | bytes 24580
  2167.8 136.3 %copy-start.99 = (f32[256]{0:T(256)S(1)}, f32[256]{0:T(256)}, u32[]{:S(2)}) copy-start(f32[256]{0:T(256)} %copy-done.98) | copy-start | bytes 3076
  2171.1 135.2 %copy-start.95 = (f32[2048]{0:T(1024)S(1)}, f32[2048]{0:T(1024)}, u32[]{:S(2)}) copy-start(f32[2048]{0:T(1024)} %get-tuple-element.716) | copy-start | bytes 24580
  2171.1 135.2 %copy-start.130 = (f32[128]{0:T(128)S(1)}, f32[128]{0:T(128)}, u32[]{:S(2)}) copy-start(f32[128]{0:T(128)} %get-tuple-element.714) | copy-start | bytes 1540
  2171.1 286.1 %copy-start.76 = (f32[2048]{0:T(1024)S(1)}, f32[2048]{0:T(1024)}, u32[]{:S(2)}) copy-start(f32[2048]{0:T(1024)} %copy-done.75) | copy-start | bytes 24580
  2171.1 286.1 %copy-start.97 = (f32[256]{0:T(256)S(1)}, f32[256]{0:T(256)}, u32[]{:S(2)}) copy-start(f32[256]{0:T(256)} %copy-done.96) | copy-start | bytes 3076
  2171.1 286.1 %copy-start.101 = (f32[256]{0:T(256)S(1)}, f32[256]{0:T(256)}, u32[]{:S(2)}) copy-start(f32[256]{0:T(256)} %copy-done.100) | copy-start | bytes 3076
  (91 other events, 302.3 us)
Sparse Core Ops, SparseCore 0:
  12.9 127.6 all-gather.4
  639.9 147.1 reduce-scatter.4
  790.9 123.9 all-gather.6
  917.1 123.1 all-gather.8
  1078.3 147.2 reduce-scatter.8
  1232.4 123.9 all-gather.10
  1908.4 242.8 all-reduce.36
  2154.9 149.1 reduce-scatter.10
  2308.2 148.9 reduce-scatter.6
where the time goes:
time: 2490 us; the launch traced here: 2470 us
  waiting for transfers between devices  1120 us (45%)
  matrix products  695 us (28%)
  local copies, waits for them, and re-layouts  292 us (12%)
  other arithmetic  292 us (12%)
  blocking collectives  55.6 us (2%)
    psum x1, waiting for transfers between devices, shards(): lax.psum(mixer_grads[0].astype(jnp.bfloat16), 'dp').astype(jnp.float32)  151 us
    reduce_scatter x1, waiting for transfers between devices, shards(): lax.psum_scatter((jnp.einsum('sf,df->sd', grad_gate, w_gate, preferred_el...  147 us
    reduce_scatter x1, waiting for transfers between devices, shards(): lax.psum_scatter(jnp.dot(mixed_low, w_out, preferred_element_type=jnp.flo...  147 us
    squeeze x192, local copies, waits for them, and re-layouts, delta_rule(): lax.scan(jax.checkpoint(advance), start_memory, (query_blocks, key_blocks...  141 us
    another operation x4, other arithmetic, delta_rule(): lax.linalg.triangular_solve(system, beta_blocks[:, :, None] * value_block...  134 us
    reduce_scatter x1, waiting for transfers between devices, shards(): lax.psum_scatter(summed.astype(jnp.bfloat16), 'tensor', scatter_dimension...  133 us
    all_gather x1, waiting for transfers between devices, shards(): ffn_full = lax.all_gather(ffn_in, 'tensor', axis=0, tiled=True)  123 us
    all_gather x1, waiting for transfers between devices, shards(): normed_full = lax.all_gather(normed, 'tensor', axis=0, tiled=True)  119 us
  transfers between devices with their start and end apart: 9, of which 9 were waited for; matrix products, arithmetic and copies ran while one was open for 7% of the time, Pallas kernels for 0%

commit v1 on v0

--- a/solution.py
+++ b/solution.py
@@ -314,7 +314,9 @@
         grad_w_out,
     )
     summed_all = (
-        lax.psum(mixer_grads[0].astype(jnp.bfloat16), "dp").astype(jnp.float32),
+        jnp.sum(lax.all_gather(mixer_grads[0].astype(jnp.bfloat16), "dp"), axis=0).astype(
+            jnp.float32
+        ),
         lax.psum(mixer_grads[1].astype(jnp.bfloat16), "dp").astype(jnp.float32),
         lax.psum(mixer_grads[2].astype(jnp.bfloat16), "dp").astype(jnp.float32),
         lax.psum(mixer_grads[3].astype(jnp.bfloat16), "dp").astype(jnp.float32),

time: 2490 us -> 2490 us (level)
  transfers between devices with their start and end apart: 9 -> 10, of which waited for: 9 -> 9; matrix products, arithmetic and copies ran while one was open for 7% -> 8% of each run, Pallas kernels for 0% -> 0%
where the time goes in v1:
time: 2490 us; the launch traced here: 2460 us
  waiting for transfers between devices  1100 us (44%)
  matrix products  695 us (28%)
  local copies, waits for them, and re-layouts  300 us (12%)
  other arithmetic  294 us (12%)
  blocking collectives  55.5 us (2%)
    reduce_scatter x1, waiting for transfers between devices, shards(): lax.psum_scatter((jnp.einsum('sf,df->sd', grad_gate, w_gate, preferred_el...  147 us
    reduce_scatter x1, waiting for transfers between devices, shards(): lax.psum_scatter(jnp.dot(mixed_low, w_out, preferred_element_type=jnp.flo...  147 us
    squeeze x192, local copies, waits for them, and re-layouts, delta_rule(): lax.scan(jax.checkpoint(advance), start_memory, (query_blocks, key_blocks...  141 us
    reduce_scatter x1, waiting for transfers between devices, shards(): lax.psum_scatter(summed.astype(jnp.bfloat16), 'tensor', scatter_dimension...  134 us
    another operation x4, other arithmetic, delta_rule(): lax.linalg.triangular_solve(system, beta_blocks[:, :, None] * value_block...  134 us
    psum x1, waiting for transfers between devices, shards(): lax.psum(mixer_grads[1].astype(jnp.bfloat16), 'dp').astype(jnp.float32)  134 us
    all_gather x1, waiting for transfers between devices, shards(): ffn_full = lax.all_gather(ffn_in, 'tensor', axis=0, tiled=True)  123 us
    all_gather x1, waiting for transfers between devices, shards(): normed_full = lax.all_gather(normed, 'tensor', axis=0, tiled=True)  119 us
  transfers between devices with their start and end apart: 10, of which 9 were waited for; matrix products, arithmetic and copies ran while one was open for 8% of the time, Pallas kernels for 0%

profile of v1, /device:TPU:0, one launch (start us, length us, event | category | flops | bytes accessed | tf_op | source)
XLA Modules:
  0.0 2464.9 jit_solution(8878827422464059386)
XLA Ops:
  14.5 4.0 copy.315
  21.9 118.7 %all-gather.7.cloned.1.call-done = bf16[2048,2048]{1,0:T(8,128)(2,1)} async-done(((bf16[256,2048]{1,0:T(8,128)(2,1)}), bf16[2048,2048]{1,0:T(8,128)(2,1)}) %all-gather.7.cloned.1.call-update) | async-done | bytes 8388624 | tf_op jit(solution)/shard_map/all_gather | solution.py:194
  140.6 5.7 fusion.50
  147.0 7.4 fusion.140
  157.5 6.0 fusion.137
  171.3 6.1 fusion.138
  177.4 6.5 fusion.135
  184.0 6.3 multiply_reduce_fusion.16
  211.6 3.9 copy.322
  215.5 5.6 copy.314
  224.4 9.4 multiply_bitcast_fusion
  233.7 133.9 %custom-call.14 = f32[2,32,1,64,64]{1,3,4,2,0:T(8,128)} custom-call(f32[2,32,1,64,64]{1,4,3,2,0:T(8,128)} %get-tuple-element.854), custom_call_target="InvertDiagBlocksLowerTriangular" | custom-call | tf_op jit(solution)/shard_map/jvp(vmap())/triangular_solve/custom-call.1 | solution.py:72
  367.7 5.6 copy.318
  373.3 4.3 fusion.61
  383.6 4.1 copy.327
  389.3 235.4 %while.40 = (s32[]{:T(128)}, f32[2,128,128]{2,1,0:T(8,128)S(1)}, f32[32,2,64,128]{3,2,0,1:T(8,128)}, f32[32,2,128,128]{3,2,1,0:T(8,128)}, f32[32]{0:T(128)S(1)},...) while((s32[]{:T(128)}, f32[2,128,128]{2,1,0:T(8,128)S(1)}, ...), condition=%wide.region_5.7_spmd.clone, body=%wide.region_4.6_spmd.clone.sunk | while | flops 88358912 | bytes 1512373 | solution.py:106
  632.5 7.3 convolution_convert_fusion.1
  640.4 146.7 %reduce-scatter.5.cloned.1.call-done = bf16[256,2048]{1,0:T(8,128)(2,1)} async-done(((bf16[2048,2048]{1,0:T(8,128)(2,1)}), bf16[256,2048]{1,0:T(8,128)(2,1)}) %reduce-scatter.5.cloned.1.call-update) | async-done | bytes 1048592 | tf_op jit(solution)/shard_map/reduce_scatter | solution.py:239
  791.4 123.5 %all-gather.9.cloned.1.call-done = bf16[2048,2048]{1,0:T(8,128)(2,1)} async-done(((bf16[256,2048]{1,0:T(8,128)(2,1)}), bf16[2048,2048]{1,0:T(8,128)(2,1)}) %all-gather.9.cloned.1.call-update) | async-done | bytes 8388624 | tf_op jit(solution)/shard_map/all_gather | solution.py:249
  914.9 11.3 fusion.142
  926.2 8.0 fusion.141
  934.2 106.0 %all-gather.11.cloned.1.call-done = bf16[2048,2048]{1,0:T(8,128)(2,1)} async-done(((bf16[256,2048]{1,0:T(8,128)(2,1)}), bf16[2048,2048]{1,0:T(8,128)(2,1)}) %all-gather.11.cloned.1.call-update) | async-done | bytes 8388624 | tf_op jit(solution)/shard_map/all_gather | solution.py:261
  1040.2 14.7 multiply_convert_fusion
  1054.9 10.7 fusion.143
  1065.6 12.5 add_convert_fusion.1
  1078.2 147.3 %reduce-scatter.9.cloned.1.call-done = bf16[256,2048]{1,0:T(8,128)(2,1)} async-done(((bf16[2048,2048]{1,0:T(8,128)(2,1)}), bf16[256,2048]{1,0:T(8,128)(2,1)}) %reduce-scatter.9.cloned.1.call-update) | async-done | bytes 1048592 | tf_op jit(solution)/shard_map/reduce_scatter | solution.py:270
  1235.1 4.6 copy.348
  1239.7 5.4 copy.337
  1245.1 10.7 convolution_convert_fusion.2
  1255.8 11.0 convolution_convert_fusion.3
  1266.8 7.5 convolution_convert_fusion.4
  1274.3 82.1 %all-gather.13.cloned.1.call-done = bf16[2048,2048]{1,0:T(8,128)(2,1)} async-done(((bf16[256,2048]{1,0:T(8,128)(2,1)}), bf16[2048,2048]{1,0:T(8,128)(2,1)}) %all-gather.13.cloned.1.call-update) | async-done | bytes 8388624 | tf_op jit(solution)/shard_map/all_gather | solution.py:281
  1356.4 7.3 fusion.144
  1366.6 5.4 multiply_reduce_fusion.1
  1382.7 380.1 %while.41 = (s32[]{:T(128)}, f32[2,128,128]{2,1,0:T(8,128)S(1)}, f32[32,2,64,128]{3,2,0,1:T(8,128)}, f32[32,2,64,128]{3,2,0,1:T(8,128)}, f32[32,2,64,128]{3,2,1,...) while((s32[]{:T(128)}, f32[2,128,128]{2,1,0:T(8,128)S(1)}, ...), condition=%wide.region_14.16_spmd.clone, body=%wide.region_13.15_spmd.clone.sunk | while | flops 201637888 | bytes 3902479 | solution.py:106
  1762.8 5.8 fusion.92
  1772.2 3.7 fusion.62
  1775.9 3.8 broadcast_multiply_fusion.1
  1786.5 5.6 copy.359
  1792.1 5.6 copy.354
  1797.7 8.1 broadcast_multiply_fusion
  1805.8 4.5 copy.361
  1810.3 5.1 fusion.148
  1826.9 10.2 fusion.79
  1852.1 9.2 multiply_reduce_fusion.9
  1866.4 6.5 multiply_reduce_fusion.4
  1877.3 3.7 convolution_convert_fusion.9
  1895.1 7.5 convolution_convert_fusion.5
  1902.6 3.7 convolution_convert_fusion.6
  1906.3 3.8 convolution_convert_fusion.7
  1914.5 8.2 fusion.133
  1922.8 8.2 fusion.150
  1931.0 8.2 fusion.151
  1939.1 8.2 fusion.145
  1947.4 26.3 %add_convert_fusion = bf16[2048,2048]{1,0:T(8,128)(2,1)} fusion(f32[2048,2048]{1,0:T(8,128)} %fusion.133, f32[2048,2048]{1,0:T(8,128)} %fusion.151, f32[2048,2048]{1,0:T(8,128)} %fusion.145, f32[2048,2048]{1,0:T(8,128)} %fusion.150, bf16[2048,256]{0,1:T(8,128)(2,1)S(1)} %bitcast.473, bf16[2048,256]{1,0:T(8,128)(2,1)S(1)} %copy-done.65), kind=kOutput, calls=%fused_computation.70 | convolution fusion | flops 2168455168 | bytes 77594624 | tf_op jit(solution)/shard_map/sh,dh->sd/dot_general | solution.py:294
  1974.0 11.2 convolution_convert_fusion
  1985.3 4.7 convolution_convert_fusion.10
  1989.9 12.5 all-reduce.33
  2004.8 4.1 reduce_sum.294
  2011.6 133.9 %all-reduce.37.cloned.1.call-done = (bf16[2048,256]{1,0:T(8,128)(2,1)}, bf16[2048,256]{1,0:T(8,128)(2,1)}, bf16[2048,256]{1,0:T(8,128)(2,1)}, bf16[256,2048]{1,0...) async-done(((bf16[2048,256]{1,0:T(8,128)(2,1)}, bf16[2048,256]{1,0:T(8,128)(2,1)}, bf16[2048,256]{1,0:T(8,128)(2,1)}, ...) | async-done | bytes 12845072 | tf_op jit(solution)/shard_map/psum | solution.py:320
  2164.2 134.3 %reduce-scatter.11.cloned.1.call-done = bf16[256,2048]{1,0:T(8,128)(2,1)} async-done(((bf16[2048,2048]{1,0:T(8,128)(2,1)}), bf16[256,2048]{1,0:T(8,128)(2,1)}) %reduce-scatter.11.cloned.1.call-update) | async-done | bytes 1048592 | tf_op jit(solution)/shard_map/reduce_scatter | solution.py:297
  2300.7 43.0 %all-reduce.32 = (f32[2048]{0:T(1024)}, f32[128]{0:T(128)}, f32[2048]{0:T(1024)}) all-reduce(f32[2048]{0:T(1024)S(1)} %get-tuple-element.718, f32[128]{0:T(128)S(1)} %copy-done.136, f32[2048]{0:T(1024)S(1)} %copy-done.101), channel_id=1, replica_groups=mesh['dp'=4,'tensor'=8] {'dp','tensor'}, use_global_device_ids=true, to_apply=%region_23.27 | all-reduce | flops 4224 | bytes 33792 | tf_op jit(solution)/shard_map/psum | solution.py:302
  2343.7 107.7 %reduce-scatter.7.cloned.1.call-done = bf16[256,2048]{1,0:T(8,128)(2,1)} async-done(((bf16[2048,2048]{1,0:T(8,128)(2,1)}), bf16[256,2048]{1,0:T(8,128)(2,1)}) %reduce-scatter.7.cloned.1.call-update) | async-done | bytes 1048592 | tf_op jit(solution)/shard_map/reduce_scatter | solution.py:255
  2451.4 6.4 fusion.55
  (1220 shorter events, 792.7 us)
Async XLA Ops:
  7.2 1033.0 %copy-start = (bf16[704,2048]{1,0:T(8,128)(2,1)S(1)}, bf16[704,2048]{1,0:T(8,128)(2,1)}, u32[]{:S(2)}) copy-start(bf16[704,2048]{1,0:T(8,128)(2,1)} %param.44) | copy-start | bytes 8650756
  7.2 133.3 %all-gather.7.cloned.1.call-start = ((), (), s32[]{:S(2)}) async-start(), calls=%async_computation.4 | async-start | bytes 9437184 | tf_op jit(solution)/shard_map/all_gather | solution.py:194
  12.8 774.3 %reduce-scatter.5.cloned.1.call-start = ((), (), s32[]{:S(2)}) async-start(), calls=%async_computation.5 | async-start | bytes 9437184 | tf_op jit(solution)/shard_map/reduce_scatter | solution.py:239
  13.2 127.4 %copy-start.99 = (bf16[2048,2]{0,1:T(2,128)(2,1)S(1)}, bf16[2048,2]{0,1:T(2,128)(2,1)}, u32[]{:S(2)}) copy-start(bf16[2048,2]{0,1:T(2,128)(2,1)} %param.37) | copy-start | bytes 24580
  19.5 204.8 %copy-start.75 = (f32[64,64]{1,0:T(8,128)}, f32[64,64]{1,0:T(8,128)S(1)}, u32[]{:S(2)}) copy-start(f32[64,64]{1,0:T(8,128)S(1)} %fusion.110) | copy-start | bytes 49156
  19.5 204.8 %copy-start.79 = (f32[64,64]{1,0:T(8,128)}, f32[64,64]{1,0:T(8,128)S(1)}, u32[]{:S(2)}) copy-start(f32[64,64]{1,0:T(8,128)S(1)} %fusion.109) | copy-start | bytes 49156
  20.0 164.0 %copy-start.122 = (f32[1,256]{1,0:T(1,128)}, f32[1,256]{1,0:T(1,128)S(1)}, u32[]{:S(2)}) copy-start(f32[1,256]{1,0:T(1,128)S(1)} %get-tuple-element.878) | copy-start | bytes 3076
  20.0 164.0 %copy-start.124 = (f32[1,256]{1,0:T(1,128)}, f32[1,256]{1,0:T(1,128)S(1)}, u32[]{:S(2)}) copy-start(f32[1,256]{1,0:T(1,128)S(1)} %get-tuple-element.880) | copy-start | bytes 3076
  20.0 164.0 %copy-start.126 = (f32[1,256]{1,0:T(1,128)}, f32[1,256]{1,0:T(1,128)S(1)}, u32[]{:S(2)}) copy-start(f32[1,256]{1,0:T(1,128)S(1)} %get-tuple-element.879) | copy-start | bytes 3076
  20.0 164.0 %copy-start.128 = (f32[1,256]{1,0:T(1,128)}, f32[1,256]{1,0:T(1,128)S(1)}, u32[]{:S(2)}) copy-start(f32[1,256]{1,0:T(1,128)S(1)} %get-tuple-element.881) | copy-start | bytes 3076
  20.0 163.9 %copy-start.108 = (f32[1,256]{1,0:T(1,128)}, f32[1,256]{1,0:T(1,128)S(1)}, u32[]{:S(2)}) copy-start(f32[1,256]{1,0:T(1,128)S(1)} %get-tuple-element.886) | copy-start | bytes 3076
  20.1 163.9 %copy-start.110 = (f32[1,256]{1,0:T(1,128)}, f32[1,256]{1,0:T(1,128)S(1)}, u32[]{:S(2)}) copy-start(f32[1,256]{1,0:T(1,128)S(1)} %get-tuple-element.888) | copy-start | bytes 3076
  20.1 163.9 %copy-start.112 = (f32[1,256]{1,0:T(1,128)}, f32[1,256]{1,0:T(1,128)S(1)}, u32[]{:S(2)}) copy-start(f32[1,256]{1,0:T(1,128)S(1)} %get-tuple-element.887) | copy-start | bytes 3076
  20.1 163.9 %copy-start.114 = (f32[1,256]{1,0:T(1,128)}, f32[1,256]{1,0:T(1,128)S(1)}, u32[]{:S(2)}) copy-start(f32[1,256]{1,0:T(1,128)S(1)} %get-tuple-element.889) | copy-start | bytes 3076
  20.1 143.4 %copy-start.116 = (f32[1,256]{1,0:T(1,128)}, f32[1,256]{1,0:T(1,128)S(1)}, u32[]{:S(2)}) copy-start(f32[1,256]{1,0:T(1,128)S(1)} %get-tuple-element.882) | copy-start | bytes 3076
  20.1 143.4 %copy-start.118 = (f32[1,256]{1,0:T(1,128)}, f32[1,256]{1,0:T(1,128)S(1)}, u32[]{:S(2)}) copy-start(f32[1,256]{1,0:T(1,128)S(1)} %get-tuple-element.883) | copy-start | bytes 3076
  20.1 143.4 %copy-start.120 = (f32[1,256]{1,0:T(1,128)}, f32[1,256]{1,0:T(1,128)S(1)}, u32[]{:S(2)}) copy-start(f32[1,256]{1,0:T(1,128)S(1)} %get-tuple-element.884) | copy-start | bytes 3076
  20.1 143.4 %copy-start.130 = (f32[1,256]{1,0:T(1,128)}, f32[1,256]{1,0:T(1,128)S(1)}, u32[]{:S(2)}) copy-start(f32[1,256]{1,0:T(1,128)S(1)} %get-tuple-element.885) | copy-start | bytes 3076
  20.2 204.1 %copy-start.97 = (pred[64,64]{1,0:T(8,128)(4,1)}, pred[64,64]{1,0:T(8,128)(4,1)S(1)}, u32[]{:S(2)}) copy-start(pred[64,64]{1,0:T(8,128)(4,1)S(1)} %iota_compare_fusion.1) | copy-start | bytes 12292
  21.0 163.0 %copy-start.91 = (f32[2048]{0:T(1024)}, f32[2048]{0:T(1024)S(1)}, u32[]{:S(2)}) copy-start(f32[2048]{0:T(1024)S(1)} %get-tuple-element.875) | copy-start | bytes 24580
  21.0 163.0 %copy-start.93 = (f32[2048]{0:T(1024)}, f32[2048]{0:T(1024)S(1)}, u32[]{:S(2)}) copy-start(f32[2048]{0:T(1024)S(1)} %get-tuple-element.877) | copy-start | bytes 24580
  21.1 163.0 %copy-start.95 = (f32[2048]{0:T(1024)}, f32[2048]{0:T(1024)S(1)}, u32[]{:S(2)}) copy-start(f32[2048]{0:T(1024)S(1)} %get-tuple-element.876) | copy-start | bytes 24580
  146.9 230.7 %copy-start.63 = (f32[2,32,64]{2,1,0:T(8,128)}, f32[2,32,64]{2,1,0:T(8,128)S(1)}, u32[]{:S(2)}) copy-start(f32[2,32,64]{2,1,0:T(8,128)S(1)} %mul.1002) | copy-start | bytes 49156
  147.0 77.3 %copy-start.73 = (f32[2,32,64]{1,2,0:T(8,128)}, f32[2,32,64]{1,2,0:T(8,128)S(1)}, u32[]{:S(2)}) copy-start(f32[2,32,64]{1,2,0:T(8,128)S(1)} %copy.312) | copy-start | bytes 49156
  639.8 275.1 %all-gather.9.cloned.1.call-start = ((), (), s32[]{:S(2)}) async-start(), calls=%async_computation.6 | async-start | bytes 9437184 | tf_op jit(solution)/shard_map/all_gather | solution.py:249
  640.4 588.5 %copy-start.81 = (f32[2048]{0:T(1024)}, f32[2048]{0:T(1024)S(1)}, u32[]{:S(2)}) copy-start(f32[2048]{0:T(1024)S(1)} %convert_element_type.276) | copy-start | bytes 24580
  789.3 439.6 %copy-start.102 = (f32[256]{0:T(256)}, f32[256]{0:T(256)S(1)}, u32[]{:S(2)}) copy-start(f32[256]{0:T(256)S(1)} %add_rsqrt_fusion.2) | copy-start | bytes 3076
  790.8 249.4 %all-gather.11.cloned.1.call-start = ((), (), s32[]{:S(2)}) async-start(), calls=%async_computation.8 | async-start | bytes 9437184 | tf_op jit(solution)/shard_map/all_gather | solution.py:261
  791.4 434.2 %reduce-scatter.9.cloned.1.call-start = ((), (), s32[]{:S(2)}) async-start(), calls=%async_computation.9 | async-start | bytes 9437184 | tf_op jit(solution)/shard_map/reduce_scatter | solution.py:270
  914.9 11.3 copy-start.138
  914.9 11.3 copy-start.139
  1040.2 14.7 copy-start.140
  1054.9 10.7 copy-start.144
  1054.9 10.7 copy-start.146
  1054.9 10.7 copy-start.141
  1078.1 278.2 %all-gather.13.cloned.1.call-start = ((), (), s32[]{:S(2)}) async-start(), calls=%async_computation.10 | async-start | bytes 9437184 | tf_op jit(solution)/shard_map/all_gather | solution.py:281
  1232.3 772.6 %all-gather.15.cloned.1.call-start = ((), (), s32[]{:S(2)}) async-start(), calls=%async_computation.12 | async-start | bytes 5242880 | tf_op jit(solution)/shard_map/all_gather | solution.py:317
  1245.1 10.7 copy-start.145
  1245.1 21.7 slice-start.4
  1255.8 11.0 slice-start.5
  1255.8 11.0 copy-start.147
  1826.9 16.1 copy-start.86
  1826.9 16.1 copy-start.88
  1852.1 9.2 copy-start.129
  1852.1 12.3 copy-start.92
  1852.1 12.3 copy-start.94
  1881.0 264.6 %all-reduce.37.cloned.1.call-start = ((), (), s32[]{:S(2)}) async-start(), calls=%async_computation.13 | async-start | bytes 25690112 | tf_op jit(solution)/shard_map/psum | solution.py:320
  1887.5 18.8 copy-start.56
  1893.9 8.7 slice-start.2
  1895.1 15.0 copy-start.58
  1913.8 384.6 %reduce-scatter.11.cloned.1.call-start = ((), (), s32[]{:S(2)}) async-start(), calls=%async_computation.11 | async-start | bytes 9437184 | tf_op jit(solution)/shard_map/reduce_scatter | solution.py:297
  1914.5 8.2 copy-start.59
  1914.5 8.2 copy-start.67
  1922.8 8.2 copy-start.68
  1939.1 8.2 copy-start.53
  1939.1 8.2 copy-start.65
  1973.7 477.7 %reduce-scatter.7.cloned.1.call-start = ((), (), s32[]{:S(2)}) async-start(), calls=%async_computation.7 | async-start | bytes 9437184 | tf_op jit(solution)/shard_map/reduce_scatter | solution.py:255
  2160.8 137.6 %copy-start.90 = (f32[2048]{0:T(1024)S(1)}, f32[2048]{0:T(1024)}, u32[]{:S(2)}) copy-start(f32[2048]{0:T(1024)} %copy-done.89) | copy-start | bytes 24580
  2160.8 137.6 %copy-start.105 = (f32[256]{0:T(256)S(1)}, f32[256]{0:T(256)}, u32[]{:S(2)}) copy-start(f32[256]{0:T(256)} %copy-done.104) | copy-start | bytes 3076
  2164.1 136.5 %copy-start.101 = (f32[2048]{0:T(1024)S(1)}, f32[2048]{0:T(1024)}, u32[]{:S(2)}) copy-start(f32[2048]{0:T(1024)} %get-tuple-element.716) | copy-start | bytes 24580
  2164.1 136.5 %copy-start.136 = (f32[128]{0:T(128)S(1)}, f32[128]{0:T(128)}, u32[]{:S(2)}) copy-start(f32[128]{0:T(128)} %get-tuple-element.714) | copy-start | bytes 1540
  2164.1 287.2 %copy-start.82 = (f32[2048]{0:T(1024)S(1)}, f32[2048]{0:T(1024)}, u32[]{:S(2)}) copy-start(f32[2048]{0:T(1024)} %copy-done.81) | copy-start | bytes 24580
  2164.1 287.2 %copy-start.103 = (f32[256]{0:T(256)S(1)}, f32[256]{0:T(256)}, u32[]{:S(2)}) copy-start(f32[256]{0:T(256)} %copy-done.102) | copy-start | bytes 3076
  2164.2 287.2 %copy-start.107 = (f32[256]{0:T(256)S(1)}, f32[256]{0:T(256)}, u32[]{:S(2)}) copy-start(f32[256]{0:T(256)} %copy-done.106) | copy-start | bytes 3076
  (100 other events, 347.8 us)
Sparse Core Ops, SparseCore 0:
  12.9 127.6 all-gather.6
  639.9 147.1 reduce-scatter.4
  790.9 123.9 all-gather.8
  917.1 123.1 all-gather.10
  1078.3 147.2 reduce-scatter.8
  1232.4 123.9 all-gather.12
  1881.1 32.6 all-gather.14
  1918.2 227.3 all-reduce.36
  2149.2 149.1 reduce-scatter.10
  2302.4 148.9 reduce-scatter.6
